TPU v7x, 128 devices: a whole 4x4x4 slice. The times are simulated.
128 devices in a mesh: pix: 32 (over y, z, core), freq: 4 (over x).
Axes of the slice: x: 4, y: 4, z: 4, core: 2. Of those that a mesh axis runs over, the one named last changes fastest.
Arguments:
- cube: float32 [1024, 65536], P('freq', 'pix'), may hold values from -6 to 6
- probes: float32 [32, 65536], P(None, 'pix'), may hold values from -6 to 6
- galaxy: float32 [65536], P('pix'), may hold values from -6 to 6
- slices: int32 [65536], P('pix'), may hold values from 0 to 127
- valid: int32 [65536], P('pix'), may hold values 0 or 1
Outputs:
- cleaned: float32 [1024, 65536], P('freq', 'pix')
- cross: float32 [1024, 128], P('freq')
All inputs are finite; a program needn't handle non-finite values. No bound on the sum of `valid` on one device may be relied on, other than what follows from the above.
Results may differ from a plain program's by a relative error of at most 0.00019.
Values sent between devices are 32-bit elements; how exact they have to be, the bound alone decides.
No kernel may reach another device: no remote copies, remote signals or barrier semaphores. Data moves between devices by JAX's collectives and lax.ppermute only.
A program may use at most 64 MiB of HBM per device.

v0:
```python
import jax
import jax.numpy as jnp
from jax import lax
from jax.sharding import PartitionSpec as P

NS = 128
ITERS = 4


def prefix(value, axis, join, neutral):
    count, mine = (lax.axis_size(axis), lax.axis_index(axis))
    pieces = lax.all_gather(value, axis)
    total = jnp.full_like(value, 0) + jnp.asarray(neutral, value.dtype)

    def lap(position, total):
        longer = join(total, pieces[position])
        return jnp.where(position < mine, longer, total)

    return lax.fori_loop(0, count - 1, lap, total)


def broadcast(value, axis, source):
    kept = jnp.where(lax.axis_index(axis) == source, value, 0).astype(value.dtype)
    return lax.psum(kept, axis)


def multiply(left, right):
    return jnp.dot(left, right, precision=lax.Precision.HIGHEST, preferred_element_type=jnp.float32)


def orthonormal(factor):
    gram = multiply(factor.T, factor)
    lower = jnp.linalg.cholesky(gram)
    return lax.linalg.triangular_solve(lower, factor, left_side=False, lower=True, transpose_a=True)


def combine_add(earlier, later):
    return earlier + later


def total_pix(term):
    before = prefix(term, "pix", combine_add, jnp.zeros_like(term))
    return broadcast(before + term, "pix", lax.axis_size("pix") - 1)


def fold_freq(term):
    return lax.psum_scatter(term, "freq", scatter_dimension=0, tiled=True)


def gather_rows(term):
    return lax.all_gather(term, "freq", axis=0, tiled=True)


def slice_table(slices, weights):
    levels = jnp.arange(NS, dtype=jnp.int32)
    return (slices[:, None] == levels[None, :]).astype(jnp.float32) * weights[:, None]


def body(cube, probes, galaxy, slices, valid):
    pixels = lax.axis_size("pix") * cube.shape[1]
    factor_scale = (float(pixels) / float(NS)) ** (-0.5)
    weights = galaxy * valid.astype(jnp.float32)
    own = lax.axis_index("freq")
    local = lax.all_to_all(cube, "freq", split_axis=1, concat_axis=0, tiled=True)
    width = local.shape[1]
    start = own * width
    probe_cols = lax.dynamic_slice_in_dim(probes, start, width, 1)
    own_weights = lax.dynamic_slice_in_dim(weights, start, width, 0)
    own_slices = lax.dynamic_slice_in_dim(slices, start, width, 0)
    basis = orthonormal(gather_rows(total_pix(fold_freq(multiply(local, probe_cols.T)))))
    for step in range(ITERS):
        amps = multiply(basis.T, local)
        basis = orthonormal(gather_rows(total_pix(fold_freq(multiply(local, amps.T)))))
    amps = multiply(basis.T, local)
    cleaned_local = local - multiply(basis, amps)
    table = slice_table(own_slices, own_weights)
    cross = total_pix(fold_freq(multiply(cleaned_local, table))) * factor_scale
    cleaned = lax.all_to_all(cleaned_local, "freq", split_axis=0, concat_axis=1, tiled=True)
    return (cleaned, cross)


def solution(mesh):
    in_specs = (P("freq", "pix"), P(None, "pix"), P("pix"), P("pix"), P("pix"))
    out_specs = (P("freq", "pix"), P("freq", None))
    return jax.shard_map(body, mesh=mesh, in_specs=in_specs, out_specs=out_specs, check_vma=False)
```

profile of v0, /device:TPU:1, one launch (start us, length us, event | category | flops | bytes accessed | tf_op | source)
XLA Modules:
  0.0 1482.5 jit_solution(6170851042177497390)
XLA Ops:
  10.4 4.8 all-to-all-start
  15.2 25.5 %all-to-all-done = f32[256,4,512]{2,0,1:T(8,128)S(1)} async-done(((f32[256,4,512]{2,0,1:T(8,128)}), f32[256,4,512]{2,0,1:T(8,128)S(1)}, u32[]{:S(2)}, u32[]{:S(2)}) %all-to-all-start) | async-done | bytes 2097184 | tf_op jit(solution)/shard_map/all_to_all | solution.py:64
  43.4 20.1 %reduce-scatter.7.cloned.1.call-done = f32[256,32]{0,1:T(8,128)} async-done(((f32[1024,32]{0,1:T(8,128)}), f32[256,32]{0,1:T(8,128)}) %reduce-scatter.7.cloned.1.call-update) | async-done | bytes 32784 | tf_op jit(solution)/shard_map/reduce_scatter | solution.py:47
  63.6 47.6 %all-gather.13.cloned.1.call-done = f32[8192,32]{0,1:T(8,128)} async-done(((f32[256,32]{0,1:T(8,128)}), f32[8192,32]{0,1:T(8,128)}) %all-gather.13.cloned.1.call-update) | async-done | bytes 1048592 | tf_op jit(solution)/shard_map/all_gather | solution.py:12
  114.7 30.1 %while.84 = (s32[]{:T(128)}, f32[256,32]{1,0:T(8,128)S(1)}, s32[]{:T(128)}, f32[32,256,32]{2,1,0:T(8,128)}, s32[]{:T(128)}, /*index=5*/s32[]{:T(128)}) while((s32[]{:T(128)}, f32[256,32]{1,0:T(8,128)S(1)}, s32[]{:T(128)}, f32[32,256,32]{2,1,0:T(8,128)}, s32[]{:T(128)}, /*index=5*/s32[]{:T(128)}) %tuple.222), condition=%wide.region_2.3_spmd.clone, body=%wide.region_1.2_spmd.clone.sunk | while | flops 24580 | bytes 98397 | solution.py:19
  144.9 120.9 %psum.42 = f32[256,32]{0,1:T(8,128)S(1)} all-reduce(f32[256,32]{0,1:T(8,128)S(1)} %add_select_fusion.11), channel_id=1, replica_groups=mesh['pix'=32,'freq'=4] {'pix'}, use_global_device_ids=true, to_apply=%region_3.4 | all-reduce | flops 8192 | bytes 65536 | tf_op jit(solution)/shard_map/psum | solution.py:24
  265.7 9.7 all_gather.53
  286.8 21.6 %reduce-scatter.9.cloned.1.call-done = f32[256,32]{0,1:T(8,128)} async-done(((f32[1024,32]{0,1:T(8,128)}), f32[256,32]{0,1:T(8,128)}) %reduce-scatter.9.cloned.1.call-update) | async-done | bytes 32784 | tf_op jit(solution)/shard_map/reduce_scatter | solution.py:47
  308.6 47.4 %all-gather.15.cloned.1.call-done = f32[8192,32]{0,1:T(8,128)} async-done(((f32[256,32]{0,1:T(8,128)}), f32[8192,32]{0,1:T(8,128)}) %all-gather.15.cloned.1.call-update) | async-done | bytes 1048592 | tf_op jit(solution)/shard_map/all_gather | solution.py:12
  359.5 30.1 %while.85 = (s32[]{:T(128)}, f32[256,32]{1,0:T(8,128)S(1)}, s32[]{:T(128)}, f32[32,256,32]{2,1,0:T(8,128)}, s32[]{:T(128)}, /*index=5*/s32[]{:T(128)}) while((s32[]{:T(128)}, f32[256,32]{1,0:T(8,128)S(1)}, s32[]{:T(128)}, f32[32,256,32]{2,1,0:T(8,128)}, s32[]{:T(128)}, /*index=5*/s32[]{:T(128)}) %tuple.223), condition=%wide.region_8.11_spmd.clone, body=%wide.region_7.10_spmd.clone.sunk | while | flops 24580 | bytes 98397 | solution.py:19
  389.7 120.9 %psum.43 = f32[256,32]{0,1:T(8,128)S(1)} all-reduce(f32[256,32]{0,1:T(8,128)S(1)} %add_select_fusion.10), channel_id=1, replica_groups=mesh['pix'=32,'freq'=4] {'pix'}, use_global_device_ids=true, to_apply=%region_9.12 | all-reduce | flops 8192 | bytes 65536 | tf_op jit(solution)/shard_map/psum | solution.py:24
  510.6 9.7 all_gather.56
  531.7 21.6 %reduce-scatter.11.cloned.1.call-done = f32[256,32]{0,1:T(8,128)} async-done(((f32[1024,32]{0,1:T(8,128)}), f32[256,32]{0,1:T(8,128)}) %reduce-scatter.11.cloned.1.call-update) | async-done | bytes 32784 | tf_op jit(solution)/shard_map/reduce_scatter | solution.py:47
  553.4 47.4 %all-gather.17.cloned.1.call-done = f32[8192,32]{0,1:T(8,128)} async-done(((f32[256,32]{0,1:T(8,128)}), f32[8192,32]{0,1:T(8,128)}) %all-gather.17.cloned.1.call-update) | async-done | bytes 1048592 | tf_op jit(solution)/shard_map/all_gather | solution.py:12
  604.4 30.1 %while.86 = (s32[]{:T(128)}, f32[256,32]{1,0:T(8,128)S(1)}, s32[]{:T(128)}, f32[32,256,32]{2,1,0:T(8,128)}, s32[]{:T(128)}, /*index=5*/s32[]{:T(128)}) while((s32[]{:T(128)}, f32[256,32]{1,0:T(8,128)S(1)}, s32[]{:T(128)}, f32[32,256,32]{2,1,0:T(8,128)}, s32[]{:T(128)}, /*index=5*/s32[]{:T(128)}) %tuple.224), condition=%wide.region_12.15_spmd.clone, body=%wide.region_11.14_spmd.clone.sunk | while | flops 24580 | bytes 98397 | solution.py:19
  634.5 120.9 %psum.44 = f32[256,32]{0,1:T(8,128)S(1)} all-reduce(f32[256,32]{0,1:T(8,128)S(1)} %add_select_fusion.9), channel_id=1, replica_groups=mesh['pix'=32,'freq'=4] {'pix'}, use_global_device_ids=true, to_apply=%region_13.16 | all-reduce | flops 8192 | bytes 65536 | tf_op jit(solution)/shard_map/psum | solution.py:24
  755.4 9.9 all_gather.59
  776.7 21.7 %reduce-scatter.13.cloned.1.call-done = f32[256,32]{0,1:T(8,128)} async-done(((f32[1024,32]{0,1:T(8,128)}), f32[256,32]{0,1:T(8,128)}) %reduce-scatter.13.cloned.1.call-update) | async-done | bytes 32784 | tf_op jit(solution)/shard_map/reduce_scatter | solution.py:47
  798.4 47.5 %all-gather.19.cloned.1.call-done = f32[8192,32]{0,1:T(8,128)} async-done(((f32[256,32]{0,1:T(8,128)}), f32[8192,32]{0,1:T(8,128)}) %all-gather.19.cloned.1.call-update) | async-done | bytes 1048592 | tf_op jit(solution)/shard_map/all_gather | solution.py:12
  849.5 30.1 %while.87 = (s32[]{:T(128)}, f32[256,32]{1,0:T(8,128)S(1)}, s32[]{:T(128)}, f32[32,256,32]{2,1,0:T(8,128)}, s32[]{:T(128)}, /*index=5*/s32[]{:T(128)}) while((s32[]{:T(128)}, f32[256,32]{1,0:T(8,128)S(1)}, s32[]{:T(128)}, f32[32,256,32]{2,1,0:T(8,128)}, s32[]{:T(128)}, /*index=5*/s32[]{:T(128)}) %tuple.225), condition=%wide.region_16.19_spmd.clone, body=%wide.region_15.18_spmd.clone.sunk | while | flops 24580 | bytes 98397 | solution.py:19
  879.6 120.9 %psum.45 = f32[256,32]{0,1:T(8,128)S(1)} all-reduce(f32[256,32]{0,1:T(8,128)S(1)} %add_select_fusion.8), channel_id=1, replica_groups=mesh['pix'=32,'freq'=4] {'pix'}, use_global_device_ids=true, to_apply=%region_17.20 | all-reduce | flops 8192 | bytes 65536 | tf_op jit(solution)/shard_map/psum | solution.py:24
  1000.5 9.7 all_gather.62
  1021.6 21.6 %reduce-scatter.15.cloned.1.call-done = f32[256,32]{0,1:T(8,128)} async-done(((f32[1024,32]{0,1:T(8,128)}), f32[256,32]{0,1:T(8,128)}) %reduce-scatter.15.cloned.1.call-update) | async-done | bytes 32784 | tf_op jit(solution)/shard_map/reduce_scatter | solution.py:47
  1044.9 45.8 %all-gather.21.cloned.1.call-done = f32[8192,32]{0,1:T(8,128)} async-done(((f32[256,32]{0,1:T(8,128)}), f32[8192,32]{0,1:T(8,128)}) %all-gather.21.cloned.1.call-update) | async-done | bytes 1048592 | tf_op jit(solution)/shard_map/all_gather | solution.py:12
  1094.3 30.1 %while.88 = (s32[]{:T(128)}, f32[256,32]{1,0:T(8,128)S(1)}, s32[]{:T(128)}, f32[32,256,32]{2,1,0:T(8,128)}, s32[]{:T(128)}, /*index=5*/s32[]{:T(128)}) while((s32[]{:T(128)}, f32[256,32]{1,0:T(8,128)S(1)}, s32[]{:T(128)}, f32[32,256,32]{2,1,0:T(8,128)}, s32[]{:T(128)}, /*index=5*/s32[]{:T(128)}) %tuple.226), condition=%wide.region_20.23_spmd.clone, body=%wide.region_19.22_spmd.clone.sunk | while | flops 24580 | bytes 98397 | solution.py:19
  1124.4 120.9 %psum.46 = f32[256,32]{0,1:T(8,128)S(1)} all-reduce(f32[256,32]{0,1:T(8,128)S(1)} %add_select_fusion.7), channel_id=1, replica_groups=mesh['pix'=32,'freq'=4] {'pix'}, use_global_device_ids=true, to_apply=%region_21.24 | all-reduce | flops 8192 | bytes 65536 | tf_op jit(solution)/shard_map/psum | solution.py:24
  1245.3 9.9 all_gather.65
  1269.8 22.6 %reduce-scatter.17.cloned.1.call-done = f32[256,128]{1,0:T(8,128)} async-done(((f32[1024,128]{1,0:T(8,128)}), f32[256,128]{1,0:T(8,128)}) %reduce-scatter.17.cloned.1.call-update) | async-done | bytes 131088 | tf_op jit(solution)/shard_map/reduce_scatter | solution.py:47
  1292.4 3.6 all-to-all-start.1
  1296.1 47.1 %all-gather.23.cloned.1.call-done = f32[8192,128]{1,0:T(8,128)} async-done(((f32[256,128]{1,0:T(8,128)}), f32[8192,128]{1,0:T(8,128)}) %all-gather.23.cloned.1.call-update) | async-done | bytes 4194320 | tf_op jit(solution)/shard_map/all_gather | solution.py:12
  1343.3 30.0 %while.89 = (s32[]{:T(128)}, f32[256,128]{1,0:T(8,128)S(1)}, s32[]{:T(128)}, f32[32,256,128]{2,1,0:T(8,128)}, s32[]{:T(128)}, /*index=5*/s32[]{:T(128)}) while((s32[]{:T(128)}, f32[256,128]{1,0:T(8,128)S(1)}, s32[]{:T(128)}, f32[32,256,128]{2,1,0:T(8,128)}, s32[]{:T(128)}, /*index=5*/s32[]{:T(128)}) %tuple.227), condition=%wide.region_24.27_spmd.clone, body=%wide.region_23.26_spmd.clone.sunk | while | flops 98308 | bytes 393309 | solution.py:19
  1375.6 98.8 %all-reduce.2.cloned.1.call-done = f32[256,128]{1,0:T(8,128)} async-done(((f32[256,128]{1,0:T(8,128)}), f32[256,128]{1,0:T(8,128)}) %all-reduce.2.cloned.1.call-update) | async-done | bytes 131088 | tf_op jit(solution)/shard_map/psum | solution.py:24
  (313 shorter events, 266.1 us)
Async XLA Ops:
  7.2 33.5 %copy-start = (f32[32,2048]{1,0:T(8,128)S(1)}, f32[32,2048]{1,0:T(8,128)}, u32[]{:S(2)}) copy-start(f32[32,2048]{1,0:T(8,128)} %param.21) | copy-start | bytes 786436
  10.4 30.3 %all-to-all-start = ((f32[256,4,512]{2,0,1:T(8,128)}), f32[256,4,512]{2,0,1:T(8,128)S(1)}, u32[]{:S(2)}, u32[]{:S(2)}) async-start(f32[256,4,512]{2,0,1:T(8,128)} %bitcast.156), calls=%async_computation | async-start | bytes 4194304 | tf_op jit(solution)/shard_map/all_to_all | solution.py:64
  15.2 48.3 %reduce-scatter.7.cloned.1.call-start = ((), (), s32[]{:S(2)}) async-start(), calls=%async_computation.8 | async-start | bytes 163840 | tf_op jit(solution)/shard_map/reduce_scatter | solution.py:47
  43.4 67.8 %all-gather.13.cloned.1.call-start = ((), (), s32[]{:S(2)}) async-start(), calls=%async_computation.15 | async-start | bytes 1081344 | tf_op jit(solution)/shard_map/all_gather | solution.py:12
  63.5 245.0 %reduce-scatter.9.cloned.1.call-start = ((), (), s32[]{:S(2)}) async-start(), calls=%async_computation.9 | async-start | bytes 163840 | tf_op jit(solution)/shard_map/reduce_scatter | solution.py:47
  114.7 30.1 %copy-start.3 = (f32[256,32]{0,1:T(8,128)S(1)}, f32[256,32]{0,1:T(8,128)}, u32[]{:S(2)}) copy-start(f32[256,32]{0,1:T(8,128)} %reduce-scatter.7.cloned.1.call-done) | copy-start | bytes 98308
  286.8 69.2 %all-gather.15.cloned.1.call-start = ((), (), s32[]{:S(2)}) async-start(), calls=%async_computation.16 | async-start | bytes 1081344 | tf_op jit(solution)/shard_map/all_gather | solution.py:12
  308.5 244.8 %reduce-scatter.11.cloned.1.call-start = ((), (), s32[]{:S(2)}) async-start(), calls=%async_computation.10 | async-start | bytes 163840 | tf_op jit(solution)/shard_map/reduce_scatter | solution.py:47
  359.5 30.1 %copy-start.5 = (f32[256,32]{0,1:T(8,128)S(1)}, f32[256,32]{0,1:T(8,128)}, u32[]{:S(2)}) copy-start(f32[256,32]{0,1:T(8,128)} %reduce-scatter.9.cloned.1.call-done) | copy-start | bytes 98308
  531.6 69.2 %all-gather.17.cloned.1.call-start = ((), (), s32[]{:S(2)}) async-start(), calls=%async_computation.17 | async-start | bytes 1081344 | tf_op jit(solution)/shard_map/all_gather | solution.py:12
  553.3 245.0 %reduce-scatter.13.cloned.1.call-start = ((), (), s32[]{:S(2)}) async-start(), calls=%async_computation.11 | async-start | bytes 163840 | tf_op jit(solution)/shard_map/reduce_scatter | solution.py:47
  604.3 30.1 %copy-start.6 = (f32[256,32]{0,1:T(8,128)S(1)}, f32[256,32]{0,1:T(8,128)}, u32[]{:S(2)}) copy-start(f32[256,32]{0,1:T(8,128)} %reduce-scatter.11.cloned.1.call-done) | copy-start | bytes 98308
  776.6 69.3 %all-gather.19.cloned.1.call-start = ((), (), s32[]{:S(2)}) async-start(), calls=%async_computation.18 | async-start | bytes 1081344 | tf_op jit(solution)/shard_map/all_gather | solution.py:12
  798.3 244.9 %reduce-scatter.15.cloned.1.call-start = ((), (), s32[]{:S(2)}) async-start(), calls=%async_computation.12 | async-start | bytes 163840 | tf_op jit(solution)/shard_map/reduce_scatter | solution.py:47
  849.5 30.1 %copy-start.7 = (f32[256,32]{0,1:T(8,128)S(1)}, f32[256,32]{0,1:T(8,128)}, u32[]{:S(2)}) copy-start(f32[256,32]{0,1:T(8,128)} %reduce-scatter.13.cloned.1.call-done) | copy-start | bytes 98308
  1021.6 69.1 %all-gather.21.cloned.1.call-start = ((), (), s32[]{:S(2)}) async-start(), calls=%async_computation.19 | async-start | bytes 1081344 | tf_op jit(solution)/shard_map/all_gather | solution.py:12
  1043.3 249.1 %reduce-scatter.17.cloned.1.call-start = ((), (), s32[]{:S(2)}) async-start(), calls=%async_computation.13 | async-start | bytes 655360 | tf_op jit(solution)/shard_map/reduce_scatter | solution.py:47
  1094.3 30.1 %copy-start.4 = (f32[256,32]{0,1:T(8,128)S(1)}, f32[256,32]{0,1:T(8,128)}, u32[]{:S(2)}) copy-start(f32[256,32]{0,1:T(8,128)} %reduce-scatter.15.cloned.1.call-done) | copy-start | bytes 98308
  1265.7 1.3 copy-start.1
  1269.8 73.5 %all-gather.23.cloned.1.call-start = ((), (), s32[]{:S(2)}) async-start(), calls=%async_computation.20 | async-start | bytes 4325376 | tf_op jit(solution)/shard_map/all_gather | solution.py:12
  1292.4 81.6 %all-to-all-start.1 = ((f32[4,256,512]{2,1,0:T(8,128)}), f32[4,256,512]{2,1,0:T(8,128)S(1)}, u32[]{:S(2)}, u32[]{:S(2)}) async-start(f32[4,256,512]{2,1,0:T(8,128)} %bitcast.154), calls=%async_computation.6 | async-start | bytes 4194304 | tf_op jit(solution)/shard_map/all_to_all | solution.py:78
  1296.1 77.2 %copy-start.2 = (f32[256,128]{1,0:T(8,128)S(1)}, f32[256,128]{1,0:T(8,128)}, u32[]{:S(2)}) copy-start(f32[256,128]{1,0:T(8,128)} %reduce-scatter.17.cloned.1.call-done) | copy-start | bytes 393220
  1296.1 178.3 %all-reduce.2.cloned.1.call-start = ((), (), s32[]{:S(2)}) async-start(), calls=%async_computation.14 | async-start | bytes 262144 | tf_op jit(solution)/shard_map/psum | solution.py:24
Sparse Core Ops, SparseCore 0:
  43.5 19.9 reduce-scatter.6
  65.7 45.4 all-gather.12
  286.9 21.5 reduce-scatter.8
  310.5 45.4 all-gather.14
  531.7 21.5 reduce-scatter.10
  555.3 45.4 all-gather.16
  776.7 21.5 reduce-scatter.12
  800.5 45.3 all-gather.18
  1021.7 21.5 reduce-scatter.14
  1045.3 45.3 all-gather.20
  1269.9 22.4 reduce-scatter.16
  1294.5 48.6 all-gather.22
  1374.1 100.2 all-reduce.1
where the time goes:
time: 1490 us; the launch traced here: 1480 us
  blocking collectives  653 us (44%)
  waiting for transfers between devices  537 us (36%)
  other arithmetic  213 us (14%)
  matrix products  27.3 us (2%)
  local copies, waits for them, and re-layouts  25.4 us (2%)
    psum x5, blocking collectives, broadcast(): return lax.psum(kept, axis)  604 us
    all_gather x6, waiting for transfers between devices, prefix(): pieces = lax.all_gather(value, axis)  283 us
    select_n x186, other arithmetic, lap(): return jnp.where(position < mine, longer, total)  176 us
    reduce_scatter x6, waiting for transfers between devices, fold_freq(): return lax.psum_scatter(term, 'freq', scatter_dimension=0, tiled=True)  129 us
    psum x1, waiting for transfers between devices, broadcast(): return lax.psum(kept, axis)  98.8 us
    all_gather x5, blocking collectives, gather_rows(): return lax.all_gather(term, 'freq', axis=0, tiled=True)  48.9 us
  transfers between devices with their start and end apart: 15, of which 14 were waited for; matrix products, arithmetic and copies ran while one was open for 2% of the time, Pallas kernels for 0%

commit v1 on v0

--- a/solution.py
+++ b/solution.py
@@ -48,7 +48,9 @@
 
 
 def gather_rows(term):
-    return lax.all_gather(term, "freq", axis=0, tiled=True)
+    return jnp.concatenate(
+        lax.all_to_all(jnp.stack([term] * lax.axis_size("freq")), "freq", 0, 0), axis=0
+    )
 
 
 def slice_table(slices, weights):

time: 1490 us -> 1470 us (0.987)
    all_gather x5 -> x0, blocking collectives: 48.9 us -> none  [gather_rows(): return lax.all_gather(term, 'freq', axis=0, tiled=True)]
    all_to_all x0 -> x4, blocking collectives: none -> 34.4 us  [gather_rows(): lax.all_to_all(jnp.stack([term] * lax.axis_size('freq')), 'freq', 0, 0)]
  transfers between devices with their start and end apart: 15 -> 16, of which waited for: 14 -> 15; matrix products, arithmetic and copies ran while one was open for 2% -> 2% of each run, Pallas kernels for 0% -> 0%
where the time goes in v1:
time: 1470 us
  blocking collectives  639 us (43%)
  waiting for transfers between devices  530 us (36%)
  other arithmetic  213 us (14%)
  matrix products  27.1 us (2%)
  local copies, waits for them, and re-layouts  26.3 us (2%)
    psum x5, blocking collectives, broadcast(): return lax.psum(kept, axis)  604 us
    all_gather x6, waiting for transfers between devices, prefix(): pieces = lax.all_gather(value, axis)  284 us
    select_n x186, other arithmetic, lap(): return jnp.where(position < mine, longer, total)  176 us
    reduce_scatter x6, waiting for transfers between devices, fold_freq(): return lax.psum_scatter(term, 'freq', scatter_dimension=0, tiled=True)  117 us
    psum x1, waiting for transfers between devices, broadcast(): return lax.psum(kept, axis)  98.8 us
    all_to_all x4, blocking collectives, gather_rows(): lax.all_to_all(jnp.stack([term] * lax.axis_size('freq')), 'freq', 0, 0)  34.4 us
  transfers between devices with their start and end apart: 16, of which 15 were waited for; matrix products, arithmetic and copies ran while one was open for 2% of the time, Pallas kernels for 0%

profile of v1, /device:TPU:1, one launch (start us, length us, event | category | flops | bytes accessed | tf_op | source)
XLA Modules:
  0.0 1465.7 jit_solution(13363620796860672328)
XLA Ops:
  10.4 4.8 all-to-all-start
  15.2 25.5 %all-to-all-done = f32[256,4,512]{2,0,1:T(8,128)S(1)} async-done(((f32[256,4,512]{2,0,1:T(8,128)}), f32[256,4,512]{2,0,1:T(8,128)S(1)}, u32[]{:S(2)}, u32[]{:S(2)}) %all-to-all-start) | async-done | bytes 2097184 | tf_op jit(solution)/shard_map/all_to_all | solution.py:66
  43.4 20.1 %reduce-scatter.7.cloned.1.call-done = f32[256,32]{0,1:T(8,128)} async-done(((f32[1024,32]{0,1:T(8,128)}), f32[256,32]{0,1:T(8,128)}) %reduce-scatter.7.cloned.1.call-update) | async-done | bytes 32784 | tf_op jit(solution)/shard_map/reduce_scatter | solution.py:47
  63.6 47.6 %all-gather.13.cloned.1.call-done = f32[8192,32]{0,1:T(8,128)} async-done(((f32[256,32]{0,1:T(8,128)}), f32[8192,32]{0,1:T(8,128)}) %all-gather.13.cloned.1.call-update) | async-done | bytes 1048592 | tf_op jit(solution)/shard_map/all_gather | solution.py:12
  114.7 30.1 %while.84 = (s32[]{:T(128)}, f32[256,32]{1,0:T(8,128)S(1)}, s32[]{:T(128)}, f32[32,256,32]{2,1,0:T(8,128)}, s32[]{:T(128)}, /*index=5*/s32[]{:T(128)}) while((s32[]{:T(128)}, f32[256,32]{1,0:T(8,128)S(1)}, s32[]{:T(128)}, f32[32,256,32]{2,1,0:T(8,128)}, s32[]{:T(128)}, /*index=5*/s32[]{:T(128)}) %tuple.227), condition=%wide.region_2.3_spmd.clone, body=%wide.region_1.2_spmd.clone.sunk | while | flops 24580 | bytes 98397 | solution.py:19
  144.9 120.9 %psum.42 = f32[256,32]{0,1:T(8,128)S(1)} all-reduce(f32[256,32]{0,1:T(8,128)S(1)} %add_select_fusion.11), channel_id=1, replica_groups=mesh['pix'=32,'freq'=4] {'pix'}, use_global_device_ids=true, to_apply=%region_3.4 | all-reduce | flops 8192 | bytes 65536 | tf_op jit(solution)/shard_map/psum | solution.py:24
  265.7 8.6 all_to_all.63
  285.8 19.3 %reduce-scatter.9.cloned.1.call-done = f32[256,32]{0,1:T(8,128)} async-done(((f32[1024,32]{0,1:T(8,128)}), f32[256,32]{0,1:T(8,128)}) %reduce-scatter.9.cloned.1.call-update) | async-done | bytes 32784 | tf_op jit(solution)/shard_map/reduce_scatter | solution.py:47
  305.1 47.4 %all-gather.15.cloned.1.call-done = f32[8192,32]{0,1:T(8,128)} async-done(((f32[256,32]{0,1:T(8,128)}), f32[8192,32]{0,1:T(8,128)}) %all-gather.15.cloned.1.call-update) | async-done | bytes 1048592 | tf_op jit(solution)/shard_map/all_gather | solution.py:12
  356.1 30.1 %while.85 = (s32[]{:T(128)}, f32[256,32]{1,0:T(8,128)S(1)}, s32[]{:T(128)}, f32[32,256,32]{2,1,0:T(8,128)}, s32[]{:T(128)}, /*index=5*/s32[]{:T(128)}) while((s32[]{:T(128)}, f32[256,32]{1,0:T(8,128)S(1)}, s32[]{:T(128)}, f32[32,256,32]{2,1,0:T(8,128)}, s32[]{:T(128)}, /*index=5*/s32[]{:T(128)}) %tuple.228), condition=%wide.region_8.11_spmd.clone, body=%wide.region_7.10_spmd.clone.sunk | while | flops 24580 | bytes 98397 | solution.py:19
  386.2 120.9 %psum.43 = f32[256,32]{0,1:T(8,128)S(1)} all-reduce(f32[256,32]{0,1:T(8,128)S(1)} %add_select_fusion.10), channel_id=1, replica_groups=mesh['pix'=32,'freq'=4] {'pix'}, use_global_device_ids=true, to_apply=%region_9.12 | all-reduce | flops 8192 | bytes 65536 | tf_op jit(solution)/shard_map/psum | solution.py:24
  507.1 8.6 all_to_all.64
  527.1 19.3 %reduce-scatter.11.cloned.1.call-done = f32[256,32]{0,1:T(8,128)} async-done(((f32[1024,32]{0,1:T(8,128)}), f32[256,32]{0,1:T(8,128)}) %reduce-scatter.11.cloned.1.call-update) | async-done | bytes 32784 | tf_op jit(solution)/shard_map/reduce_scatter | solution.py:47
  546.5 47.4 %all-gather.17.cloned.1.call-done = f32[8192,32]{0,1:T(8,128)} async-done(((f32[256,32]{0,1:T(8,128)}), f32[8192,32]{0,1:T(8,128)}) %all-gather.17.cloned.1.call-update) | async-done | bytes 1048592 | tf_op jit(solution)/shard_map/all_gather | solution.py:12
  597.5 30.1 %while.86 = (s32[]{:T(128)}, f32[256,32]{1,0:T(8,128)S(1)}, s32[]{:T(128)}, f32[32,256,32]{2,1,0:T(8,128)}, s32[]{:T(128)}, /*index=5*/s32[]{:T(128)}) while((s32[]{:T(128)}, f32[256,32]{1,0:T(8,128)S(1)}, s32[]{:T(128)}, f32[32,256,32]{2,1,0:T(8,128)}, s32[]{:T(128)}, /*index=5*/s32[]{:T(128)}) %tuple.229), condition=%wide.region_12.15_spmd.clone, body=%wide.region_11.14_spmd.clone.sunk | while | flops 24580 | bytes 98397 | solution.py:19
  627.6 120.9 %psum.44 = f32[256,32]{0,1:T(8,128)S(1)} all-reduce(f32[256,32]{0,1:T(8,128)S(1)} %add_select_fusion.9), channel_id=1, replica_groups=mesh['pix'=32,'freq'=4] {'pix'}, use_global_device_ids=true, to_apply=%region_13.16 | all-reduce | flops 8192 | bytes 65536 | tf_op jit(solution)/shard_map/psum | solution.py:24
  748.5 8.6 all_to_all.65
  768.6 19.2 %reduce-scatter.13.cloned.1.call-done = f32[256,32]{0,1:T(8,128)} async-done(((f32[1024,32]{0,1:T(8,128)}), f32[256,32]{0,1:T(8,128)}) %reduce-scatter.13.cloned.1.call-update) | async-done | bytes 32784 | tf_op jit(solution)/shard_map/reduce_scatter | solution.py:47
  787.9 47.5 %all-gather.19.cloned.1.call-done = f32[8192,32]{0,1:T(8,128)} async-done(((f32[256,32]{0,1:T(8,128)}), f32[8192,32]{0,1:T(8,128)}) %all-gather.19.cloned.1.call-update) | async-done | bytes 1048592 | tf_op jit(solution)/shard_map/all_gather | solution.py:12
  839.0 30.1 %while.87 = (s32[]{:T(128)}, f32[256,32]{1,0:T(8,128)S(1)}, s32[]{:T(128)}, f32[32,256,32]{2,1,0:T(8,128)}, s32[]{:T(128)}, /*index=5*/s32[]{:T(128)}) while((s32[]{:T(128)}, f32[256,32]{1,0:T(8,128)S(1)}, s32[]{:T(128)}, f32[32,256,32]{2,1,0:T(8,128)}, s32[]{:T(128)}, /*index=5*/s32[]{:T(128)}) %tuple.230), condition=%wide.region_16.19_spmd.clone, body=%wide.region_15.18_spmd.clone.sunk | while | flops 24580 | bytes 98397 | solution.py:19
  869.1 120.9 %psum.45 = f32[256,32]{0,1:T(8,128)S(1)} all-reduce(f32[256,32]{0,1:T(8,128)S(1)} %add_select_fusion.8), channel_id=1, replica_groups=mesh['pix'=32,'freq'=4] {'pix'}, use_global_device_ids=true, to_apply=%region_17.20 | all-reduce | flops 8192 | bytes 65536 | tf_op jit(solution)/shard_map/psum | solution.py:24
  990.0 8.6 all_to_all.66
  1010.0 19.3 %reduce-scatter.15.cloned.1.call-done = f32[256,32]{0,1:T(8,128)} async-done(((f32[1024,32]{0,1:T(8,128)}), f32[256,32]{0,1:T(8,128)}) %reduce-scatter.15.cloned.1.call-update) | async-done | bytes 32784 | tf_op jit(solution)/shard_map/reduce_scatter | solution.py:47
  1030.1 46.6 %all-gather.21.cloned.1.call-done = f32[8192,32]{0,1:T(8,128)} async-done(((f32[256,32]{0,1:T(8,128)}), f32[8192,32]{0,1:T(8,128)}) %all-gather.21.cloned.1.call-update) | async-done | bytes 1048592 | tf_op jit(solution)/shard_map/all_gather | solution.py:12
  1080.3 30.1 %while.88 = (s32[]{:T(128)}, f32[256,32]{1,0:T(8,128)S(1)}, s32[]{:T(128)}, f32[32,256,32]{2,1,0:T(8,128)}, s32[]{:T(128)}, /*index=5*/s32[]{:T(128)}) while((s32[]{:T(128)}, f32[256,32]{1,0:T(8,128)S(1)}, s32[]{:T(128)}, f32[32,256,32]{2,1,0:T(8,128)}, s32[]{:T(128)}, /*index=5*/s32[]{:T(128)}) %tuple.231), condition=%wide.region_20.23_spmd.clone, body=%wide.region_19.22_spmd.clone.sunk | while | flops 24580 | bytes 98397 | solution.py:19
  1110.5 120.9 %psum.46 = f32[256,32]{0,1:T(8,128)S(1)} all-reduce(f32[256,32]{0,1:T(8,128)S(1)} %add_select_fusion.7), channel_id=1, replica_groups=mesh['pix'=32,'freq'=4] {'pix'}, use_global_device_ids=true, to_apply=%region_21.24 | all-reduce | flops 8192 | bytes 65536 | tf_op jit(solution)/shard_map/psum | solution.py:24
  1232.0 4.0 all-to-all-start.5
  1236.8 4.0 all-to-all-done.5
  1255.4 20.2 %reduce-scatter.17.cloned.1.call-done = f32[256,128]{1,0:T(8,128)} async-done(((f32[1024,128]{1,0:T(8,128)}), f32[256,128]{1,0:T(8,128)}) %reduce-scatter.17.cloned.1.call-update) | async-done | bytes 131088 | tf_op jit(solution)/shard_map/reduce_scatter | solution.py:47
  1279.3 47.1 %all-gather.23.cloned.1.call-done = f32[8192,128]{1,0:T(8,128)} async-done(((f32[256,128]{1,0:T(8,128)}), f32[8192,128]{1,0:T(8,128)}) %all-gather.23.cloned.1.call-update) | async-done | bytes 4194320 | tf_op jit(solution)/shard_map/all_gather | solution.py:12
  1326.5 30.0 %while.89 = (s32[]{:T(128)}, f32[256,128]{1,0:T(8,128)S(1)}, s32[]{:T(128)}, f32[32,256,128]{2,1,0:T(8,128)}, s32[]{:T(128)}, /*index=5*/s32[]{:T(128)}) while((s32[]{:T(128)}, f32[256,128]{1,0:T(8,128)S(1)}, s32[]{:T(128)}, f32[32,256,128]{2,1,0:T(8,128)}, s32[]{:T(128)}, /*index=5*/s32[]{:T(128)}) %tuple.232), condition=%wide.region_24.27_spmd.clone, body=%wide.region_23.26_spmd.clone.sunk | while | flops 98308 | bytes 393309 | solution.py:19
  1358.8 98.8 %all-reduce.2.cloned.1.call-done = f32[256,128]{1,0:T(8,128)} async-done(((f32[256,128]{1,0:T(8,128)}), f32[256,128]{1,0:T(8,128)}) %all-reduce.2.cloned.1.call-update) | async-done | bytes 131088 | tf_op jit(solution)/shard_map/psum | solution.py:24
  (324 shorter events, 270.4 us)
Async XLA Ops:
  7.2 33.5 %copy-start = (f32[32,2048]{1,0:T(8,128)S(1)}, f32[32,2048]{1,0:T(8,128)}, u32[]{:S(2)}) copy-start(f32[32,2048]{1,0:T(8,128)} %param.21) | copy-start | bytes 786436
  10.4 30.3 %all-to-all-start = ((f32[256,4,512]{2,0,1:T(8,128)}), f32[256,4,512]{2,0,1:T(8,128)S(1)}, u32[]{:S(2)}, u32[]{:S(2)}) async-start(f32[256,4,512]{2,0,1:T(8,128)} %bitcast.176), calls=%async_computation | async-start | bytes 4194304 | tf_op jit(solution)/shard_map/all_to_all | solution.py:66
  15.2 48.3 %reduce-scatter.7.cloned.1.call-start = ((), (), s32[]{:S(2)}) async-start(), calls=%async_computation.13 | async-start | bytes 163840 | tf_op jit(solution)/shard_map/reduce_scatter | solution.py:47
  43.4 67.8 %all-gather.13.cloned.1.call-start = ((), (), s32[]{:S(2)}) async-start(), calls=%async_computation.20 | async-start | bytes 1081344 | tf_op jit(solution)/shard_map/all_gather | solution.py:12
  63.5 241.5 %reduce-scatter.9.cloned.1.call-start = ((), (), s32[]{:S(2)}) async-start(), calls=%async_computation.14 | async-start | bytes 163840 | tf_op jit(solution)/shard_map/reduce_scatter | solution.py:47
  114.7 30.1 %copy-start.3 = (f32[256,32]{0,1:T(8,128)S(1)}, f32[256,32]{0,1:T(8,128)}, u32[]{:S(2)}) copy-start(f32[256,32]{0,1:T(8,128)} %reduce-scatter.7.cloned.1.call-done) | copy-start | bytes 98308
  285.7 66.8 %all-gather.15.cloned.1.call-start = ((), (), s32[]{:S(2)}) async-start(), calls=%async_computation.21 | async-start | bytes 1081344 | tf_op jit(solution)/shard_map/all_gather | solution.py:12
  305.1 241.4 %reduce-scatter.11.cloned.1.call-start = ((), (), s32[]{:S(2)}) async-start(), calls=%async_computation.15 | async-start | bytes 163840 | tf_op jit(solution)/shard_map/reduce_scatter | solution.py:47
  356.1 30.1 %copy-start.4 = (f32[256,32]{0,1:T(8,128)S(1)}, f32[256,32]{0,1:T(8,128)}, u32[]{:S(2)}) copy-start(f32[256,32]{0,1:T(8,128)} %reduce-scatter.9.cloned.1.call-done) | copy-start | bytes 98308
  527.1 66.8 %all-gather.17.cloned.1.call-start = ((), (), s32[]{:S(2)}) async-start(), calls=%async_computation.22 | async-start | bytes 1081344 | tf_op jit(solution)/shard_map/all_gather | solution.py:12
  546.4 241.4 %reduce-scatter.13.cloned.1.call-start = ((), (), s32[]{:S(2)}) async-start(), calls=%async_computation.16 | async-start | bytes 163840 | tf_op jit(solution)/shard_map/reduce_scatter | solution.py:47
  597.5 30.1 %copy-start.5 = (f32[256,32]{0,1:T(8,128)S(1)}, f32[256,32]{0,1:T(8,128)}, u32[]{:S(2)}) copy-start(f32[256,32]{0,1:T(8,128)} %reduce-scatter.11.cloned.1.call-done) | copy-start | bytes 98308
  768.5 66.9 %all-gather.19.cloned.1.call-start = ((), (), s32[]{:S(2)}) async-start(), calls=%async_computation.23 | async-start | bytes 1081344 | tf_op jit(solution)/shard_map/all_gather | solution.py:12
  787.8 241.5 %reduce-scatter.15.cloned.1.call-start = ((), (), s32[]{:S(2)}) async-start(), calls=%async_computation.17 | async-start | bytes 163840 | tf_op jit(solution)/shard_map/reduce_scatter | solution.py:47
  839.0 30.1 %copy-start.6 = (f32[256,32]{0,1:T(8,128)S(1)}, f32[256,32]{0,1:T(8,128)}, u32[]{:S(2)}) copy-start(f32[256,32]{0,1:T(8,128)} %reduce-scatter.13.cloned.1.call-done) | copy-start | bytes 98308
  1010.0 66.8 %all-gather.21.cloned.1.call-start = ((), (), s32[]{:S(2)}) async-start(), calls=%async_computation.24 | async-start | bytes 1081344 | tf_op jit(solution)/shard_map/all_gather | solution.py:12
  1080.3 30.1 %copy-start.7 = (f32[256,32]{0,1:T(8,128)S(1)}, f32[256,32]{0,1:T(8,128)}, u32[]{:S(2)}) copy-start(f32[256,32]{0,1:T(8,128)} %reduce-scatter.15.cloned.1.call-done) | copy-start | bytes 98308
  1232.0 8.8 all-to-all-start.5
  1236.0 39.6 %reduce-scatter.17.cloned.1.call-start = ((), (), s32[]{:S(2)}) async-start(), calls=%async_computation.18 | async-start | bytes 655360 | tf_op jit(solution)/shard_map/reduce_scatter | solution.py:47
  1251.3 1.3 copy-start.1
  1255.4 71.1 %all-gather.23.cloned.1.call-start = ((), (), s32[]{:S(2)}) async-start(), calls=%async_computation.25 | async-start | bytes 4325376 | tf_op jit(solution)/shard_map/all_gather | solution.py:12
  1275.7 81.6 %all-to-all-start.6 = ((f32[4,256,512]{2,1,0:T(8,128)}), f32[4,256,512]{2,1,0:T(8,128)S(1)}, u32[]{:S(2)}, u32[]{:S(2)}) async-start(f32[4,256,512]{2,1,0:T(8,128)} %bitcast.174), calls=%async_computation.11 | async-start | bytes 4194304 | tf_op jit(solution)/shard_map/all_to_all | solution.py:80
  1279.3 77.2 %copy-start.2 = (f32[256,128]{1,0:T(8,128)S(1)}, f32[256,128]{1,0:T(8,128)}, u32[]{:S(2)}) copy-start(f32[256,128]{1,0:T(8,128)} %reduce-scatter.17.cloned.1.call-done) | copy-start | bytes 393220
  1279.3 178.3 %all-reduce.2.cloned.1.call-start = ((), (), s32[]{:S(2)}) async-start(), calls=%async_computation.19 | async-start | bytes 262144 | tf_op jit(solution)/shard_map/psum | solution.py:24
Sparse Core Ops, SparseCore 0:
  43.5 19.9 reduce-scatter.6
  65.7 45.4 all-gather.12
  285.8 19.1 reduce-scatter.8
  307.1 45.3 all-gather.14
  527.2 19.1 reduce-scatter.10
  548.5 45.4 all-gather.16
  768.6 19.1 reduce-scatter.12
  790.0 45.3 all-gather.18
  1010.1 19.1 reduce-scatter.14
  1031.3 45.3 all-gather.20
  1255.5 20.0 reduce-scatter.16
  1277.7 48.6 all-gather.22
  1357.3 100.2 all-reduce.1
